TPU v7x, 32 devices: a whole 2x2x4 slice. The times are simulated.
32 devices in a mesh: coef: 16 (over z, y, x), rot: 2 (over core).
Axes of the slice: x: 2, y: 2, z: 4, core: 2. Of those that a mesh axis runs over, the one named last changes fastest.
Arguments:
- features: float32 [256, 47872], P(None, 'coef'), may hold values from -200 to 200
- table: float32 [2048, 47872], P('rot', 'coef'), may hold values from -16 to 16
- targets: float32 [256, 2048], P('coef', 'rot'), may hold values from 0 to 1
Outputs:
- grad_features: float32 [256, 47872], P('rot', 'coef')
- grad_table: float32 [2048, 47872], P('rot', 'coef')
All inputs are finite; a program needn't handle non-finite values.
Results may differ from a plain program's by a relative error of at most 0.0003.
Values sent between devices are 32-bit elements; how exact they have to be, the bound alone decides.
No kernel may reach another device: no remote copies, remote signals or barrier semaphores. Data moves between devices by JAX's collectives and lax.ppermute only.
A program may use at most 64 MiB of HBM per device.

v0:
```python
import math
import jax
import jax.numpy as jnp
from jax import lax
from jax.sharding import PartitionSpec as P

K = 47872
logit_gain = 4.0
loss_scale = 64.0


def on_device(features, table, targets):
    scale = logit_gain / math.sqrt(K)
    partial_value = lax.dot_general(
        features,
        table,
        (((1,), (1,)), ((), ())),
        precision=lax.Precision.HIGHEST,
        preferred_element_type=jnp.float32,
    )
    summed = lax.psum_scatter(partial_value, "coef", scatter_dimension=0, tiled=True)
    scores = scale * summed
    local_max = jnp.max(scores, axis=1)
    row_max = lax.pmax(local_max, "rot")
    expo = jnp.exp(scores - row_max[:, None])
    row_total = lax.psum(jnp.sum(expo, axis=1), "rot")
    probs = expo / row_total[:, None]
    grad_scores = loss_scale * (probs - targets)
    piece = lax.all_gather(grad_scores, "coef", axis=0, tiled=True)
    table_part = lax.dot_general(
        piece,
        features,
        (((0,), (0,)), ((), ())),
        precision=lax.Precision.HIGHEST,
        preferred_element_type=jnp.float32,
    )
    feature_part = jnp.dot(
        piece, table, precision=lax.Precision.HIGHEST, preferred_element_type=jnp.float32
    )
    grad_features = scale * lax.psum_scatter(feature_part, "rot", scatter_dimension=0, tiled=True)
    grad_table = scale * table_part
    return (grad_features, grad_table)


def solution(mesh):
    return jax.shard_map(
        on_device,
        mesh=mesh,
        in_specs=(P(None, "coef"), P("rot", "coef"), P("coef", "rot")),
        out_specs=(P("rot", "coef"), P("rot", "coef")),
        check_vma=False,
    )
```

profile of v0, /device:TPU:0, one launch (start us, length us, event | category | flops | bytes accessed | tf_op | source)
XLA Modules:
  0.0 202.1 jit_solution(17302437431089537872)
XLA Ops:
  7.2 0.0 copy-start
  7.2 0.0 copy-start.1
  7.2 0.0 reduce-scatter.3.cloned.1.call-start
  7.2 1.8 copy-done
  9.0 14.6 %fusion.1 = f32[256,1024]{1,0:T(8,128)} fusion(f32[256,2992]{0,1:T(8,128)S(1)} %copy-done, f32[1024,2992]{0,1:T(8,128)} %param.4), kind=kOutput, calls=%fused_computation.6 | convolution fusion | flops 9412018176 | bytes 16367616 | tf_op jit(solution)/shard_map/dot_general | solution.py:14
  23.6 0.0 reduce-scatter.3.cloned.1.call-update
  23.7 0.0 all-gather.2.cloned.1.call-start
  23.7 81.6 %reduce-scatter.3.cloned.1.call-done = f32[16,1024]{1,0:T(8,128)} async-done(((f32[256,1024]{1,0:T(8,128)}), f32[16,1024]{1,0:T(8,128)}) %reduce-scatter.3.cloned.1.call-update) | async-done | bytes 65552 | tf_op jit(solution)/shard_map/reduce_scatter | solution.py:21
  105.3 1.0 multiply_reduce_fusion
  106.3 2.5 %pmax.7 = f32[16]{0:T(128)S(1)} all-reduce(f32[16]{0:T(128)S(1)} %multiply_reduce_fusion), channel_id=1, replica_groups=mesh['coef'=16,'rot'=2] {'rot'}, use_global_device_ids=true, to_apply=%region_2.0 | all-reduce | flops 16 | bytes 128 | tf_op jit(solution)/shard_map/pmax | solution.py:24
  108.8 1.0 fusion
  109.8 2.5 %psum.7 = f32[16]{0:T(128)S(1)} all-reduce(f32[16]{0:T(128)S(1)} %fusion), channel_id=1, replica_groups=mesh['coef'=16,'rot'=2] {'rot'}, use_global_device_ids=true, to_apply=%region_4.0 | all-reduce | flops 16 | bytes 128 | tf_op jit(solution)/shard_map/psum | solution.py:26
  112.3 0.0 copy-done.1
  112.3 1.6 subtract_multiply_fusion
  113.8 0.0 all-gather.2.cloned.1.call-update
  113.8 0.2 reduce-scatter.5.cloned.1.call-start
  114.1 51.3 %all-gather.2.cloned.1.call-done = f32[256,1024]{1,0:T(8,128)} async-done(((f32[16,1024]{1,0:T(8,128)}), f32[256,1024]{1,0:T(8,128)}) %all-gather.2.cloned.1.call-update) | async-done | bytes 1048592 | tf_op jit(solution)/shard_map/all_gather | solution.py:29
  165.4 13.5 %fusion.2 = f32[256,2992]{0,1:T(8,128)} fusion(f32[256,1024]{1,0:T(8,128)} %all-gather.2.cloned.1.call-done, f32[1024,2992]{0,1:T(8,128)} %param.4), kind=kOutput, calls=%fused_computation.7 | convolution fusion | flops 9412018176 | bytes 16367616 | tf_op jit(solution)/shard_map/dot_general | solution.py:37
  178.9 0.0 reduce-scatter.5.cloned.1.call-update
  178.9 14.0 %convolution_multiply_fusion = f32[1024,2992]{0,1:T(8,128)} fusion(f32[256,1024]{1,0:T(8,128)} %all-gather.2.cloned.1.call-done, f32[256,2992]{0,1:T(8,128)S(1)} %copy-done), kind=kOutput, calls=%fused_computation | convolution fusion | flops 9415081984 | bytes 16367616 | tf_op jit(solution)/shard_map/dot_general | solution.py:30
  192.9 0.0 reduce-scatter.5.cloned.1.call-done
  192.9 2.7 %broadcast_multiply_fusion = f32[128,2992]{0,1:T(8,128)} fusion(f32[128,2992]{0,1:T(8,128)} %reduce-scatter.5.cloned.1.call-done), kind=kLoop, calls=%fused_computation.1 | loop fusion | flops 382976 | bytes 3063808 | tf_op jit(solution)/shard_map/mul | solution.py:40
Async XLA Ops:
  7.2 1.9 copy-start
  7.2 105.1 %copy-start.1 = (f32[16,1024]{1,0:T(8,128)S(1)}, f32[16,1024]{1,0:T(8,128)}, u32[]{:S(2)}) copy-start(f32[16,1024]{1,0:T(8,128)} %param.5) | copy-start | bytes 196612
  7.2 98.1 %reduce-scatter.3.cloned.1.call-start = ((), (), s32[]{:S(2)}) async-start(), calls=%async_computation.2 | async-start | bytes 1114112 | tf_op jit(solution)/shard_map/reduce_scatter | solution.py:21
  23.7 141.8 %all-gather.2.cloned.1.call-start = ((), (), s32[]{:S(2)}) async-start(), calls=%async_computation.3 | async-start | bytes 1114112 | tf_op jit(solution)/shard_map/all_gather | solution.py:29
  113.8 79.1 %reduce-scatter.5.cloned.1.call-start = ((), (), s32[]{:S(2)}) async-start(), calls=%async_computation.4 | async-start | bytes 4595712 | tf_op jit(solution)/shard_map/reduce_scatter | solution.py:40
Sparse Core Ops, SparseCore 0:
  23.8 81.4 reduce-scatter.2
  114.0 51.4 all-gather.1
  179.0 9.6 reduce-scatter.4
where the time goes:
time: 202 us
  waiting for transfers between devices  133 us (66%)
  matrix products  42.1 us (21%)
  between operations  13.8 us (7%)
  other arithmetic  6.2 us (3%)
  blocking collectives  4.93 us (2%)
    reduce_scatter x1, waiting for transfers between devices, on_device(): lax.psum_scatter(partial_value, 'coef', scatter_dimension=0, tiled=True)  81.6 us
    all_gather x1, waiting for transfers between devices, on_device(): piece = lax.all_gather(grad_scores, 'coef', axis=0, tiled=True)  51.3 us
    dot_general x1, matrix products, on_device(): lax.dot_general(features, table, (((1,), (1,)), ((), ())), precision=lax....  14.6 us
    dot_general x1, matrix products, on_device(): lax.dot_general(piece, features, (((0,), (0,)), ((), ())), precision=lax....  14 us
    dot_general x1, matrix products, on_device(): jnp.dot(piece, table, precision=lax.Precision.HIGHEST, preferred_element_...  13.5 us
  transfers between devices with their start and end apart: 3, of which 2 were waited for; matrix products, arithmetic and copies ran while one was open for 7% of the time, Pallas kernels for 0%

commit v1 on v0

--- a/solution.py
+++ b/solution.py
@@ -26,7 +26,15 @@
     row_total = lax.psum(jnp.sum(expo, axis=1), "rot")
     probs = expo / row_total[:, None]
     grad_scores = loss_scale * (probs - targets)
-    piece = lax.all_gather(grad_scores, "coef", axis=0, tiled=True)
+    ways, here, step = (lax.axis_size("coef"), lax.axis_index("coef"), grad_scores.shape[0])
+    line, have = (grad_scores, 1)
+    while have < ways:
+        line = jnp.concatenate(
+            [line, lax.ppermute(line, "coef", [(d, (d - have) % ways) for d in range(ways)])],
+            axis=0,
+        )
+        have = 2 * have
+    piece = jnp.roll(line, here * step, axis=0)
     table_part = lax.dot_general(
         piece,
         features,

time: 202 us -> 199 us (0.985)
  waiting for transfers between devices: 133 us -> 117 us
  local copies, waits for them, and re-layouts: 1.81 us -> 11.2 us
    all_gather x1 -> x0, waiting for transfers between devices: 51.3 us -> none  [on_device(): piece = lax.all_gather(grad_scores, 'coef', axis=0, tiled=True)]
    ppermute x0 -> x4, waiting for transfers between devices: none -> 34.1 us  [on_device(): lax.ppermute(line, 'coef', [(d, (d - have) % ways) for d in range(ways)])]
    unnamed x4 -> x16, local copies, waits for them, and re-layouts: 1.81 us -> 9.27 us
  transfers between devices with their start and end apart: 3 -> 6, of which waited for: 2 -> 6; matrix products, arithmetic and copies ran while one was open for 7% -> 9% of each run, Pallas kernels for 0% -> 0%
where the time goes in v1:
time: 199 us; the launch traced here: 197 us
  waiting for transfers between devices  117 us (59%)
  matrix products  42.1 us (21%)
  between operations  14.1 us (7%)
  local copies, waits for them, and re-layouts  11.2 us (6%)
  other arithmetic  7.06 us (4%)
  blocking collectives  4.93 us (2%)
    reduce_scatter x1, waiting for transfers between devices, on_device(): lax.psum_scatter(partial_value, 'coef', scatter_dimension=0, tiled=True)  81.6 us
    ppermute x4, waiting for transfers between devices, on_device(): lax.ppermute(line, 'coef', [(d, (d - have) % ways) for d in range(ways)])  34.1 us
    dot_general x1, matrix products, on_device(): lax.dot_general(features, table, (((1,), (1,)), ((), ())), precision=lax....  14.6 us
    dot_general x1, matrix products, on_device(): lax.dot_general(piece, features, (((0,), (0,)), ((), ())), precision=lax....  14 us
    dot_general x1, matrix products, on_device(): jnp.dot(piece, table, precision=lax.Precision.HIGHEST, preferred_element_...  13.5 us
    unnamed x16, local copies, waits for them, and re-layouts  9.27 us
  transfers between devices with their start and end apart: 6, of which 6 were waited for; matrix products, arithmetic and copies ran while one was open for 9% of the time, Pallas kernels for 0%

profile of v1, /device:TPU:0, one launch (start us, length us, event | category | flops | bytes accessed | tf_op | source)
XLA Modules:
  0.0 197.4 jit_solution(10452074654701648662)
XLA Ops:
  7.2 0.0 reduce-scatter.3.cloned.1.call-start
  7.2 1.8 copy-done
  9.0 14.6 %fusion.6 = f32[256,1024]{1,0:T(8,128)} fusion(f32[256,2992]{0,1:T(8,128)S(1)} %copy-done, f32[1024,2992]{0,1:T(8,128)} %param.4), kind=kOutput, calls=%fused_computation.24 | convolution fusion | flops 9412018176 | bytes 16367616 | tf_op jit(solution)/shard_map/dot_general | solution.py:14
  23.6 0.0 reduce-scatter.3.cloned.1.call-update
  23.7 0.0 reduce-scatter.5.cloned.1.call-start
  23.7 81.6 %reduce-scatter.3.cloned.1.call-done = f32[16,1024]{1,0:T(8,128)} async-done(((f32[256,1024]{1,0:T(8,128)}), f32[16,1024]{1,0:T(8,128)}) %reduce-scatter.3.cloned.1.call-update) | async-done | bytes 65552 | tf_op jit(solution)/shard_map/reduce_scatter | solution.py:21
  105.3 1.0 multiply_reduce_fusion
  106.3 2.5 %pmax.7 = f32[16]{0:T(128)S(1)} all-reduce(f32[16]{0:T(128)S(1)} %multiply_reduce_fusion), channel_id=1, replica_groups=mesh['coef'=16,'rot'=2] {'rot'}, use_global_device_ids=true, to_apply=%region_2.0 | all-reduce | flops 16 | bytes 128 | tf_op jit(solution)/shard_map/pmax | solution.py:24
  108.8 1.0 fusion.3
  109.8 2.5 %psum.7 = f32[16]{0:T(128)S(1)} all-reduce(f32[16]{0:T(128)S(1)} %fusion.3), channel_id=1, replica_groups=mesh['coef'=16,'rot'=2] {'rot'}, use_global_device_ids=true, to_apply=%region_4.0 | all-reduce | flops 16 | bytes 128 | tf_op jit(solution)/shard_map/psum | solution.py:26
  112.3 1.6 constant_dynamic-update-slice_fusion.9
  113.8 0.4 collective-permute-start
  114.2 3.9 %collective-permute-done = f32[16,1024]{1,0:T(8,128)S(1)} collective-permute-done((f32[16,1024]{1,0:T(8,128)S(1)}, f32[16,1024]{1,0:T(8,128)S(1)}, u32[]{:S(2)}, u32[]{:S(2)}) %collective-permute-start) | collective-permute-done | bytes 65568 | tf_op jit(solution)/shard_map/ppermute | solution.py:33
  118.1 0.6 collective-permute-start.1
  118.7 4.4 %collective-permute-done.1 = f32[32,1024]{1,0:T(8,128)S(1)} collective-permute-done((f32[32,1024]{1,0:T(8,128)S(1)}, f32[32,1024]{1,0:T(8,128)S(1)}, u32[]{:S(2)}, u32[]{:S(2)}) %collective-permute-start.1) | collective-permute-done | bytes 131104 | tf_op jit(solution)/shard_map/ppermute | solution.py:33
  123.1 0.2 collective-permute-start.2
  123.4 6.4 %collective-permute-done.2 = f32[64,1024]{1,0:T(8,128)S(1)} collective-permute-done((f32[64,1024]{1,0:T(8,128)S(1)}, f32[64,1024]{1,0:T(8,128)S(1)}, u32[]{:S(2)}, u32[]{:S(2)}) %collective-permute-start.2) | collective-permute-done | bytes 262176 | tf_op jit(solution)/shard_map/ppermute | solution.py:33
  129.7 0.8 pad_maximum_fusion
  130.6 1.5 constant_dynamic-update-slice_fusion.8
  132.1 0.7 constant_dynamic-update-slice_fusion.7
  132.8 0.7 constant_dynamic-update-slice_fusion.6
  133.5 19.5 %collective-permute-done.3 = f32[128,1024]{1,0:T(8,128)} collective-permute-done((f32[128,1024]{1,0:T(8,128)}, f32[128,1024]{1,0:T(8,128)}, u32[]{:S(2)}, u32[]{:S(2)}) %collective-permute-start.3) | collective-permute-done | bytes 524320 | tf_op jit(solution)/shard_map/ppermute | solution.py:33
  153.0 1.9 constant_dynamic-update-slice_fusion.5
  154.9 0.6 constant_dynamic-update-slice_fusion.4
  155.6 0.6 constant_dynamic-update-slice_fusion.3
  156.2 0.7 constant_dynamic-update-slice_fusion.2
  156.8 0.7 constant_dynamic-update-slice_fusion.1
  157.6 1.9 constant_dynamic-update-slice_fusion
  159.5 13.5 %fusion.1 = f32[256,2992]{0,1:T(8,128)} fusion(f32[1024,2992]{0,1:T(8,128)} %param.4, f32[512,1024]{1,0:T(8,128)} %constant_dynamic-update-slice_fusion, s32[]{:T(128)S(6)} %select_n.14), kind=kOutput, calls=%fused_computation.2 | convolution fusion | flops 9412018176 | bytes 16367620 | tf_op jit(solution)/shard_map/dot_general | solution.py:45
  173.0 14.0 %convolution_multiply_fusion = f32[1024,2992]{0,1:T(8,128)} fusion(f32[256,2992]{0,1:T(8,128)S(1)} %copy-done, f32[512,1024]{1,0:T(8,128)} %constant_dynamic-update-slice_fusion, s32[]{:T(128)S(6)} %select_n.14), kind=kOutput, calls=%fused_computation | convolution fusion | flops 9415081984 | bytes 16367620 | tf_op jit(solution)/shard_map/dot_general | solution.py:38
  187.0 1.0 reduce-scatter.5.cloned.1.call-done
  188.0 2.7 %broadcast_multiply_fusion = f32[128,2992]{0,1:T(8,128)} fusion(f32[128,2992]{0,1:T(8,128)} %reduce-scatter.5.cloned.1.call-done), kind=kLoop, calls=%fused_computation.4 | loop fusion | flops 382976 | bytes 3063808 | tf_op jit(solution)/shard_map/mul | solution.py:48
  (11 shorter events, 0.1 us)
Async XLA Ops:
  7.2 1.9 copy-start
  7.2 105.1 %copy-start.3 = (f32[16,1024]{1,0:T(8,128)S(1)}, f32[16,1024]{1,0:T(8,128)}, u32[]{:S(2)}) copy-start(f32[16,1024]{1,0:T(8,128)} %param.5) | copy-start | bytes 196612
  7.2 98.1 %reduce-scatter.3.cloned.1.call-start = ((), (), s32[]{:S(2)}) async-start(), calls=%async_computation.2 | async-start | bytes 1114112 | tf_op jit(solution)/shard_map/reduce_scatter | solution.py:21
  23.7 164.3 %reduce-scatter.5.cloned.1.call-start = ((), (), s32[]{:S(2)}) async-start(), calls=%async_computation.3 | async-start | bytes 4595712 | tf_op jit(solution)/shard_map/reduce_scatter | solution.py:48
  113.8 4.3 %collective-permute-start = (f32[16,1024]{1,0:T(8,128)S(1)}, f32[16,1024]{1,0:T(8,128)S(1)}, u32[]{:S(2)}, u32[]{:S(2)}) collective-permute-start(f32[16,1024]{1,0:T(8,128)S(1)} %get-tuple-element.3), channel_id=1, source_target_pairs={{0,30},{2,0},{4,2},{6,4},{8,6},{10,8},{12,10},{14,12},{16,14},{18,... | collective-permute-start | bytes 196616 | tf_op jit(solution)/shard_map/ppermute | solution.py:33
  118.1 11.7 %copy-start.1 = (f32[16,1024]{1,0:T(8,128)}, f32[16,1024]{1,0:T(8,128)S(1)}, u32[]{:S(2)}) copy-start(f32[16,1024]{1,0:T(8,128)S(1)} %collective-permute-done) | copy-start | bytes 196612
  118.1 5.0 %collective-permute-start.1 = (f32[32,1024]{1,0:T(8,128)S(1)}, f32[32,1024]{1,0:T(8,128)S(1)}, u32[]{:S(2)}, u32[]{:S(2)}) collective-permute-start(f32[32,1024]{1,0:T(8,128)S(1)} %pad_maximum_fusion.2), channel_id=1, source_target_pairs={{0,28},{2,30},{4,0},{6,2},{8,4},{10,6},{12,8},{14,10},{16,12},{18,... | collective-permute-start | bytes 393224 | tf_op jit(solution)/shard_map/ppermute | solution.py:33
  123.1 6.6 %collective-permute-start.2 = (f32[64,1024]{1,0:T(8,128)S(1)}, f32[64,1024]{1,0:T(8,128)S(1)}, u32[]{:S(2)}, u32[]{:S(2)}) collective-permute-start(f32[64,1024]{1,0:T(8,128)S(1)} %pad_maximum_fusion.1), channel_id=1, source_target_pairs={{0,24},{2,26},{4,28},{6,30},{8,0},{10,2},{12,4},{14,6},{16,8},{18,... | collective-permute-start | bytes 786440 | tf_op jit(solution)/shard_map/ppermute | solution.py:33
  130.6 22.4 %collective-permute-start.3 = (f32[128,1024]{1,0:T(8,128)}, f32[128,1024]{1,0:T(8,128)}, u32[]{:S(2)}, u32[]{:S(2)}) collective-permute-start(f32[128,1024]{1,0:T(8,128)} %pad_maximum_fusion), channel_id=1, source_target_pairs={{0,16},{2,18},{4,20},{6,22},{8,24},{10,26},{12,28},{14,30},{16,0},... | collective-permute-start | bytes 1572872 | tf_op jit(solution)/shard_map/ppermute | solution.py:33
  130.6 25.0 %copy-start.2 = (f32[16,1024]{1,0:T(8,128)S(1)}, f32[16,1024]{1,0:T(8,128)}, u32[]{:S(2)}) copy-start(f32[16,1024]{1,0:T(8,128)} %copy-done.1) | copy-start | bytes 196612
Sparse Core Ops, SparseCore 0:
  23.8 81.4 reduce-scatter.2
  173.1 14.8 reduce-scatter.4
